TPU v7x, 128 devices: a whole 4x4x4 slice. The times are simulated.
128 devices in a mesh: row: 8 (over z_hi, x), blk: 16 (over z_lo, y, core).
Axes of the slice: x: 4, y: 4, z: 4 (z_hi: 2, z_lo: 2; z = z_hi * 2 + z_lo), core: 2. Of those that a mesh axis runs over, the one named last changes fastest.
Arguments:
- spike_counts: int32 [16384, 2048], P(('row', 'blk')), may hold values from 0 to 23, as said below
- kernel_taps: int32 [16], replicated, may hold values from 1 to 8
- lag_bins: int32 [2], replicated, may hold values from 1 to 32, as said below
Outputs:
- correlogram: bfloat16 [2, 16384, 8, 2048], P(None, 'row', None, 'blk')
Inputs may be any that keep to these rules, and one draw needn't show every extreme that they name: `spike_counts`: neurons fire at different rates and share a common drive. `lag_bins`: the second lag equals 32; the first lies between 1 and 31.
All inputs are finite; a program needn't handle non-finite values.
Results may differ from a plain program's by a relative error of at most 0.0034.
Values may be sent and summed in bfloat16 or wider, within the bound.
A program may use at most 128 MiB of HBM per device.

v0:
```python
import jax
import jax.numpy as jnp
from jax import lax
from jax.sharding import PartitionSpec as P

NEURONS = 16384
BINS = 2048
TAPS = 16


def smoothed(spike_counts, kernel_taps):
    counts = spike_counts.astype(jnp.float32)
    weights = kernel_taps.astype(jnp.float32) / jnp.sum(kernel_taps.astype(jnp.float32))
    padded = jnp.pad(counts, ((0, 0), (TAPS - 1, 0)))
    result = jnp.zeros_like(counts)
    for delay in range(TAPS):
        result = result + weights[delay] * padded[:, TAPS - 1 - delay : TAPS - 1 - delay + BINS]
    return result


def later_bins(data, lag):
    padded = jnp.pad(data, ((0, 0), (0, BINS)))
    return lax.dynamic_slice_in_dim(padded, lag, BINS, 1)


def shards(spike_counts, kernel_taps, lag_bins):
    smooth = smoothed(spike_counts, kernel_taps)
    centred = smooth - jnp.mean(smooth, axis=1, keepdims=True)
    totals = lax.psum(jnp.sum(centred, axis=0), ("row", "blk"))
    residual_part = centred - (totals / NEURONS)[None, :]
    zscored = (
        residual_part
        * lax.rsqrt(jnp.mean(residual_part * residual_part, axis=1, keepdims=True) + 1e-05)
    ).astype(jnp.bfloat16)
    span_rows = zscored.shape[0]
    groups = lax.axis_size("row")
    columns = lax.all_gather(zscored, "row", axis=0, tiled=True)
    stacked = jnp.concatenate(
        [later_bins(columns, lag_bins[0]), later_bins(columns, lag_bins[1])], axis=0
    )
    piece = lax.all_gather(zscored, "blk", axis=0, tiled=True)
    product = jnp.dot(piece, stacked.T, preferred_element_type=jnp.float32) / BINS
    product = product.reshape(piece.shape[0], 2, groups, span_rows)
    return jnp.transpose(product, (1, 0, 2, 3)).astype(jnp.bfloat16)


def solution(mesh):
    placed = (P(("row", "blk"), None), P(), P())
    return jax.shard_map(
        shards, mesh=mesh, in_specs=placed, out_specs=P(None, "row", None, "blk"), check_vma=False
    )
```

profile of v0, /device:TPU:1, one launch (start us, length us, event | category | flops | bytes accessed | tf_op | source)
XLA Modules:
  0.0 258.9 jit_solution(15566849793997691235)
XLA Ops:
  6.5 0.0 copy-start
  6.5 0.0 all-gather.5.cloned.1.call-start
  6.5 1.3 convert_reduce_fusion
  7.8 1.3 convert_divide_fusion
  9.1 0.7 fusion.8
  9.8 1.3 convert_element_type.25
  11.2 14.1 %fusion.6 = (f32[128]{0:T(128)S(1)}, f32[128,2048]{1,0:T(8,128)S(1)}) fusion(f32[]{:T(128)} %bitcast.15, f32[]{:T(128)} %bitcast.14, f32[]{:T(128)} %bitcast.13, f32[]{:T(128)} %bitcast.12, f32[]{:T(128)} %bitcast.11, f32[]{:T(128)} %bitcast.10, f32[]{:T(128)} %bitcast.9, f32[]{:T(128)} %bitcast.8, f32[]{:T(128)} %bitcast.7, f32[]{:T(128)} %bitcast.6, ...), kind=kLoop, calls=%fused_computation.19 | loop fusion | flops 8388480 | bytes 2097728 | tf_op jit(solution)/shard_map/reduce_sum | solution.py:28
  25.3 0.2 subtract_reduce_fusion
  25.5 68.7 %psum.7 = f32[2048]{0:T(1024)S(1)} all-reduce(f32[2048]{0:T(1024)S(1)} %subtract_reduce_fusion), channel_id=1, replica_groups=mesh['row'=8,'blk'=16] {'row','blk'}, use_global_device_ids=true, to_apply=%region_3.4 | all-reduce | flops 2048 | bytes 16384 | tf_op jit(solution)/shard_map/psum | solution.py:29
  94.2 0.3 multiply_reduce_fusion
  94.5 1.0 multiply_convert_fusion.1
  95.5 0.0 all-gather.5.cloned.1.call-update
  95.6 0.2 all-gather.3.cloned.1.call-start
  95.8 0.5 all-gather.3.cloned.1.call-update
  96.3 0.0 copy-done
  96.3 0.6 fusion.7
  100.7 62.5 %all-gather.5.cloned.1.call-done = bf16[1024,2048]{1,0:T(8,128)(2,1)} async-done(((bf16[128,2048]{1,0:T(8,128)(2,1)}), bf16[1024,2048]{1,0:T(8,128)(2,1)}) %all-gather.5.cloned.1.call-update) | async-done | bytes 4194320 | tf_op jit(solution)/shard_map/all_gather | solution.py:37
  163.2 10.0 %pad_dynamic-slice_fusion.1 = (bf16[1024,2048]{1,0:T(8,128)(2,1)}, bf16[1024,2048]{1,0:T(8,128)(2,1)}) fusion(s32[]{:T(128)S(6)} %select_n.6, bf16[1024,2048]{1,0:T(8,128)(2,1)} %all-gather.5.cloned.1.call-done, s32[]{:T(128)S(6)} %select_n.7), kind=kLoop, calls=%fused_computation.2 | loop fusion | bytes 12582920 | tf_op jit(solution)/shard_map/dynamic_slice | solution.py:23
  173.2 42.5 %all-gather.3.cloned.1.call-done = bf16[2048,2048]{1,0:T(8,128)(2,1)} async-done(((bf16[128,2048]{1,0:T(8,128)(2,1)}), bf16[2048,2048]{1,0:T(8,128)(2,1)}) %all-gather.3.cloned.1.call-update) | async-done | bytes 8388624 | tf_op jit(solution)/shard_map/all_gather | solution.py:41
  215.7 23.8 %multiply_convert_fusion = bf16[2048,2048]{0,1:T(8,128)(2,1)} fusion(bf16[2048,2048]{1,0:T(8,128)(2,1)} %all-gather.3.cloned.1.call-done, bf16[1024,2048]{1,0:T(8,128)(2,1)} %get-tuple-element.8, bf16[1024,2048]{1,0:T(8,128)(2,1)} %get-tuple-element.7), kind=kOutput, calls=%fused_computation | convolution fusion | flops 17205035008 | bytes 25165824 | tf_op jit(solution)/shard_map/dot_general | solution.py:42
  239.5 12.6 %copy.4 = bf16[2048,2,8,128]{3,2,0,1:T(8,128)(2,1)} copy(bf16[2048,2,8,128]{0,3,2,1:T(8,128)(2,1)} %bitcast.21) | data formatting | bytes 16777216 | tf_op jit(solution)/shard_map/convert_element_type | solution.py:44
  (3 shorter events, 0.0 us)
Async XLA Ops:
  6.5 89.8 %copy-start = (s32[2]{0:T(128)S(1)}, s32[2]{0:T(128)}, u32[]{:S(2)}) copy-start(s32[2]{0:T(128)} %param.5) | copy-start | bytes 28
  6.5 156.7 %all-gather.5.cloned.1.call-start = ((), (), s32[]{:S(2)}) async-start(), calls=%async_computation.1 | async-start | bytes 4718592 | tf_op jit(solution)/shard_map/all_gather | solution.py:37
  95.6 120.2 %all-gather.3.cloned.1.call-start = ((), (), s32[]{:S(2)}) async-start(), calls=%async_computation | async-start | bytes 8912896 | tf_op jit(solution)/shard_map/all_gather | solution.py:41
Sparse Core Ops, SparseCore 0:
  95.7 67.5 all-gather.4
  165.0 50.7 all-gather.2
where the time goes:
time: 260 us; the launch traced here: 259 us
  waiting for transfers between devices  106 us (41%)
  blocking collectives  68.7 us (26%)
  local copies, waits for them, and re-layouts  23.9 us (9%)
  matrix products  23.8 us (9%)
  other arithmetic  19.5 us (8%)
  between operations  17.2 us (7%)
    psum x1, blocking collectives, shards(): totals = lax.psum(jnp.sum(centred, axis=0), ('row', 'blk'))  68.7 us
    all_gather x1, waiting for transfers between devices, shards(): columns = lax.all_gather(zscored, 'row', axis=0, tiled=True)  62.5 us
    all_gather x1, waiting for transfers between devices, shards(): piece = lax.all_gather(zscored, 'blk', axis=0, tiled=True)  42.5 us
    dot_general x1, matrix products, shards(): jnp.dot(piece, stacked.T, preferred_element_type=jnp.float32) / BINS  23.8 us
    reduce_sum x1, other arithmetic, shards(): centred = smooth - jnp.mean(smooth, axis=1, keepdims=True)  14.1 us
    convert_element_type x1, local copies, waits for them, and re-layouts, shards(): return jnp.transpose(product, (1, 0, 2, 3)).astype(jnp.bfloat16)  12.6 us
    dynamic_slice x1, local copies, waits for them, and re-layouts, later_bins(): return lax.dynamic_slice_in_dim(padded, lag, BINS, 1)  9.97 us
  transfers between devices with their start and end apart: 2, of which 2 were waited for; matrix products, arithmetic and copies ran while one was open for 4% of the time, Pallas kernels for 0%

commit v1 on v0

--- a/solution.py
+++ b/solution.py
@@ -1,3 +1,4 @@
+import functools
 import jax
 import jax.numpy as jnp
 from jax import lax
@@ -6,6 +7,15 @@
 NEURONS = 16384
 BINS = 2048
 TAPS = 16
+
+
+def create_cards(chunk, bus_axis, chip_axis):
+    for c in (bus_axis, chip_axis):
+        chunk = lax.psum(chunk, axis_name=c)
+    return chunk
+
+
+fill_the_node = functools.partial(create_cards, bus_axis="blk", chip_axis="row")
 
 
 def smoothed(spike_counts, kernel_taps):
@@ -26,7 +36,7 @@
 def shards(spike_counts, kernel_taps, lag_bins):
     smooth = smoothed(spike_counts, kernel_taps)
     centred = smooth - jnp.mean(smooth, axis=1, keepdims=True)
-    totals = lax.psum(jnp.sum(centred, axis=0), ("row", "blk"))
+    totals = fill_the_node(jnp.sum(centred, axis=0))
     residual_part = centred - (totals / NEURONS)[None, :]
     zscored = (
         residual_part

time: 260 us -> 245 us (0.942)
  blocking collectives: 68.7 us -> 50.3 us
  waiting for transfers between devices: 106 us -> 109 us
    psum x1 -> x2, blocking collectives: 68.7 us -> 50.3 us  [create_cards(): chunk = lax.psum(chunk, axis_name=c)]
    all_gather x1, waiting for transfers between devices: 62.5 us -> 66.5 us  [shards(): columns = lax.all_gather(zscored, 'row', axis=0, tiled=True)]
where the time goes in v1:
time: 245 us; the launch traced here: 244 us
  waiting for transfers between devices  109 us (44%)
  blocking collectives  50.3 us (21%)
  local copies, waits for them, and re-layouts  23.9 us (10%)
  matrix products  23.8 us (10%)
  other arithmetic  19.5 us (8%)
  between operations  17.2 us (7%)
    all_gather x1, waiting for transfers between devices, shards(): columns = lax.all_gather(zscored, 'row', axis=0, tiled=True)  66.5 us
    psum x2, blocking collectives, create_cards(): chunk = lax.psum(chunk, axis_name=c)  50.3 us
    all_gather x1, waiting for transfers between devices, shards(): piece = lax.all_gather(zscored, 'blk', axis=0, tiled=True)  42.5 us
    dot_general x1, matrix products, shards(): jnp.dot(piece, stacked.T, preferred_element_type=jnp.float32) / BINS  23.8 us
    reduce_sum x1, other arithmetic, shards(): centred = smooth - jnp.mean(smooth, axis=1, keepdims=True)  14.1 us
    convert_element_type x1, local copies, waits for them, and re-layouts, shards(): return jnp.transpose(product, (1, 0, 2, 3)).astype(jnp.bfloat16)  12.6 us
    dynamic_slice x1, local copies, waits for them, and re-layouts, later_bins(): return lax.dynamic_slice_in_dim(padded, lag, BINS, 1)  9.97 us
  transfers between devices with their start and end apart: 2, of which 2 were waited for; matrix products, arithmetic and copies ran while one was open for 4% of the time, Pallas kernels for 0%

profile of v1, /device:TPU:1, one launch (start us, length us, event | category | flops | bytes accessed | tf_op | source)
XLA Modules:
  0.0 244.4 jit_solution(10958570971838929804)
XLA Ops:
  6.5 0.0 copy-start
  6.5 0.0 all-gather.5.cloned.1.call-start
  6.5 1.3 convert_reduce_fusion
  7.8 1.3 convert_divide_fusion
  9.1 0.7 fusion.8
  9.8 1.3 convert_element_type.25
  11.2 14.1 %fusion.6 = (f32[128]{0:T(128)S(1)}, f32[128,2048]{1,0:T(8,128)S(1)}) fusion(f32[]{:T(128)} %bitcast.15, f32[]{:T(128)} %bitcast.14, f32[]{:T(128)} %bitcast.13, f32[]{:T(128)} %bitcast.12, f32[]{:T(128)} %bitcast.11, f32[]{:T(128)} %bitcast.10, f32[]{:T(128)} %bitcast.9, f32[]{:T(128)} %bitcast.8, f32[]{:T(128)} %bitcast.7, f32[]{:T(128)} %bitcast.6, ...), kind=kLoop, calls=%fused_computation.19 | loop fusion | flops 8388480 | bytes 2097728 | tf_op jit(solution)/shard_map/reduce_sum | solution.py:38
  25.3 0.2 subtract_reduce_fusion
  25.5 29.1 %psum.14 = f32[2048]{0:T(1024)S(1)} all-reduce(f32[2048]{0:T(1024)S(1)} %subtract_reduce_fusion), channel_id=1, replica_groups=mesh['row'=8,'blk'=16] {'blk'}, use_global_device_ids=true, to_apply=%region_3.4 | all-reduce | flops 2048 | bytes 16384 | tf_op jit(solution)/shard_map/psum | solution.py:14
  54.6 21.2 %psum.15 = f32[2048]{0:T(1024)S(1)} all-reduce(f32[2048]{0:T(1024)S(1)} %psum.14), channel_id=1, replica_groups=mesh['row'=8,'blk'=16] {'row'}, use_global_device_ids=true, to_apply=%region_4.5 | all-reduce | flops 2048 | bytes 16384 | tf_op jit(solution)/shard_map/psum | solution.py:14
  75.8 0.3 multiply_reduce_fusion
  76.1 1.0 multiply_convert_fusion.1
  77.2 0.0 all-gather.5.cloned.1.call-update
  77.2 0.2 all-gather.3.cloned.1.call-start
  77.4 0.5 all-gather.3.cloned.1.call-update
  77.9 0.0 copy-done
  77.9 0.6 fusion.7
  82.3 66.5 %all-gather.5.cloned.1.call-done = bf16[1024,2048]{1,0:T(8,128)(2,1)} async-done(((bf16[128,2048]{1,0:T(8,128)(2,1)}), bf16[1024,2048]{1,0:T(8,128)(2,1)}) %all-gather.5.cloned.1.call-update) | async-done | bytes 4194320 | tf_op jit(solution)/shard_map/all_gather | solution.py:47
  148.8 10.0 %pad_dynamic-slice_fusion.1 = (bf16[1024,2048]{1,0:T(8,128)(2,1)}, bf16[1024,2048]{1,0:T(8,128)(2,1)}) fusion(s32[]{:T(128)S(6)} %select_n.6, bf16[1024,2048]{1,0:T(8,128)(2,1)} %all-gather.5.cloned.1.call-done, s32[]{:T(128)S(6)} %select_n.7), kind=kLoop, calls=%fused_computation.2 | loop fusion | bytes 12582920 | tf_op jit(solution)/shard_map/dynamic_slice | solution.py:33
  158.8 42.5 %all-gather.3.cloned.1.call-done = bf16[2048,2048]{1,0:T(8,128)(2,1)} async-done(((bf16[128,2048]{1,0:T(8,128)(2,1)}), bf16[2048,2048]{1,0:T(8,128)(2,1)}) %all-gather.3.cloned.1.call-update) | async-done | bytes 8388624 | tf_op jit(solution)/shard_map/all_gather | solution.py:51
  201.2 23.8 %multiply_convert_fusion = bf16[2048,2048]{0,1:T(8,128)(2,1)} fusion(bf16[2048,2048]{1,0:T(8,128)(2,1)} %all-gather.3.cloned.1.call-done, bf16[1024,2048]{1,0:T(8,128)(2,1)} %get-tuple-element.8, bf16[1024,2048]{1,0:T(8,128)(2,1)} %get-tuple-element.7), kind=kOutput, calls=%fused_computation | convolution fusion | flops 17205035008 | bytes 25165824 | tf_op jit(solution)/shard_map/dot_general | solution.py:52
  225.0 12.6 %copy.4 = bf16[2048,2,8,128]{3,2,0,1:T(8,128)(2,1)} copy(bf16[2048,2,8,128]{0,3,2,1:T(8,128)(2,1)} %bitcast.21) | data formatting | bytes 16777216 | tf_op jit(solution)/shard_map/convert_element_type | solution.py:54
  (3 shorter events, 0.0 us)
Async XLA Ops:
  6.5 71.4 %copy-start = (s32[2]{0:T(128)S(1)}, s32[2]{0:T(128)}, u32[]{:S(2)}) copy-start(s32[2]{0:T(128)} %param.5) | copy-start | bytes 28
  6.5 142.3 %all-gather.5.cloned.1.call-start = ((), (), s32[]{:S(2)}) async-start(), calls=%async_computation.1 | async-start | bytes 4718592 | tf_op jit(solution)/shard_map/all_gather | solution.py:47
  77.2 124.1 %all-gather.3.cloned.1.call-start = ((), (), s32[]{:S(2)}) async-start(), calls=%async_computation | async-start | bytes 8912896 | tf_op jit(solution)/shard_map/all_gather | solution.py:51
Sparse Core Ops, SparseCore 0:
  77.3 71.4 all-gather.4
  150.5 50.7 all-gather.2
